TPU v7x, 768 devices: a whole 4x8x12 slice. The times are simulated.
768 devices in a mesh: inner: 8 (over y), outer: 24 (over x_hi, z), head: 4 (over x_lo, core).
Axes of the slice: x: 4 (x_hi: 2, x_lo: 2; x = x_hi * 2 + x_lo), y: 8, z: 12, core: 2. Of those that a mesh axis runs over, the one named last changes fastest.
Arguments:
- queries: bfloat16 [49152, 64, 128], P(('inner', 'outer', 'head')), may hold values from -6 to 6
- key_vector_rows: bfloat16 [49152, 8, 128], P(('inner', 'outer'), 'head'), may hold values from -6 to 6
- value_vector_rows: bfloat16 [49152, 8, 128], P(('inner', 'outer'), 'head'), may hold values from -6 to 6
- grad_out: bfloat16 [49152, 64, 128], P(('inner', 'outer', 'head')), may hold values from -24 to 24
Outputs:
- query_grads: bfloat16 [49152, 64, 128], P(('inner', 'outer', 'head'))
- key_gradient_rows: bfloat16 [49152, 8, 128], P(('inner', 'outer'), 'head')
- value_gradient_rows: bfloat16 [49152, 8, 128], P(('inner', 'outer'), 'head')
All inputs are finite; a program needn't handle non-finite values.
Results may differ from a plain program's by a relative error of at most 0.012.
Values may be sent and summed in bfloat16 or wider, within the bound.
A program may use at most 64 MiB of HBM per device.

v0:
```python
import jax
import jax.numpy as jnp
from jax import lax
from jax.sharding import PartitionSpec as P


def sent_together(arrays, axis, split_dim, concat_dim, along):
    ends, at = ([], 0)
    for a in arrays[:-1]:
        at += a.shape[along]
        ends.append(at)
    both = jnp.concatenate(arrays, axis=along)
    return tuple(
        jnp.split(
            lax.all_to_all(both, axis, split_axis=split_dim, concat_axis=concat_dim, tiled=True),
            ends,
            axis=along,
        )
    )


def from_behind(value, axis, by):
    peers = lax.axis_size(axis)
    pairs = [(i, i + by) for i in range(peers) if 0 <= i + by < peers]
    return lax.ppermute(value, axis, pairs)


def head_grads(query_part, grad_part, key_part, value_part, allowed):
    softmax_scale = query_part.shape[-1] ** (-0.5)
    scores = (
        jnp.einsum("rgd,kd->grk", query_part, key_part, preferred_element_type=jnp.float32)
        * softmax_scale
    )
    scores = jnp.where(allowed[None], scores, -jnp.inf)
    highest = jnp.max(scores, axis=-1, keepdims=True)
    probs = jnp.exp(scores - highest)
    probs = probs / jnp.sum(probs, axis=-1, keepdims=True)
    probs_low = probs.astype(jnp.bfloat16)
    value_gradient_rows = jnp.einsum(
        "grk,rgd->kd", probs_low, grad_part, preferred_element_type=jnp.float32
    )
    dprobs = jnp.einsum("rgd,kd->grk", grad_part, value_part, preferred_element_type=jnp.float32)
    delta = jnp.sum(probs * dprobs, axis=-1, keepdims=True)
    dscores = (probs * (dprobs - delta)).astype(jnp.bfloat16)
    query_grads = (
        jnp.einsum("grk,kd->rgd", dscores, key_part, preferred_element_type=jnp.float32)
        * softmax_scale
    )
    key_gradient_rows = (
        jnp.einsum("grk,rgd->kd", dscores, query_part, preferred_element_type=jnp.float32)
        * softmax_scale
    )
    return (query_grads, key_gradient_rows, value_gradient_rows)


def block_grads(query_rows, grad_rows, key_window, value_window, allowed):
    row_count, head_count, width = query_rows.shape
    group_count = key_window.shape[1]
    heads_per_group = head_count // group_count
    query_split = query_rows.reshape(row_count, group_count, heads_per_group, width).transpose(
        1, 0, 2, 3
    )
    grad_split = grad_rows.reshape(row_count, group_count, heads_per_group, width).transpose(
        1, 0, 2, 3
    )
    key_split = key_window.transpose(1, 0, 2)
    value_split = value_window.transpose(1, 0, 2)
    query_grads, key_gradient_rows, value_gradient_rows = lax.map(
        lambda packed: head_grads(packed[0], packed[1], packed[2], packed[3], allowed),
        (query_split, grad_split, key_split, value_split),
    )
    query_grads = query_grads.transpose(1, 0, 2, 3).reshape(row_count, head_count, width)
    return (
        query_grads,
        key_gradient_rows.transpose(1, 0, 2),
        value_gradient_rows.transpose(1, 0, 2),
    )


def shards(queries, key_vector_rows, value_vector_rows, grad_out):
    tok_rows = key_vector_rows.shape[0]
    block_index = lax.axis_index(("inner", "outer"))
    query_rows, grad_rows = sent_together((queries, grad_out), "head", 1, 0, 2)
    source = (key_vector_rows, value_vector_rows)
    query_positions = block_index * tok_rows + jnp.arange(tok_rows, dtype=jnp.int32)
    arrived = []
    for shift_by in (2, 1):
        arrived.append(from_behind((source[0], source[1]), ("inner", "outer"), shift_by))
    key_window = jnp.concatenate([arrived[0][0], arrived[1][0], source[0]], axis=0)
    value_window = jnp.concatenate([arrived[0][1], arrived[1][1], source[1]], axis=0)
    key_positions = (block_index - 2) * tok_rows + jnp.arange(3 * tok_rows, dtype=jnp.int32)
    allowed = (key_positions[None, :] <= query_positions[:, None]) & (key_positions[None, :] >= 0)
    query_grads, key_gradient_rows, value_gradient_rows = block_grads(
        query_rows, grad_rows, key_window, value_window, allowed
    )
    query_result = lax.all_to_all(
        query_grads.astype(jnp.bfloat16), "head", split_axis=0, concat_axis=1, tiled=True
    )
    key_slot_rows = key_gradient_rows.reshape(
        3, tok_rows, key_gradient_rows.shape[1], key_gradient_rows.shape[2]
    )
    value_slot_rows = value_gradient_rows.reshape(
        3, tok_rows, value_gradient_rows.shape[1], value_gradient_rows.shape[2]
    )
    key_total = key_slot_rows[2]
    value_total = value_slot_rows[2]
    for back_by in (1, 2):
        key_back, value_back = from_behind(
            (key_slot_rows[2 - back_by], value_slot_rows[2 - back_by]), ("inner", "outer"), -back_by
        )
        key_total = key_total + key_back
        value_total = value_total + value_back
    return (query_result, key_total.astype(jnp.bfloat16), value_total.astype(jnp.bfloat16))


def solution(mesh):
    return jax.shard_map(
        shards,
        mesh=mesh,
        in_specs=(
            P(("inner", "outer", "head"), None, None),
            P(("inner", "outer"), "head", None),
            P(("inner", "outer"), "head", None),
            P(("inner", "outer", "head"), None, None),
        ),
        out_specs=(
            P(("inner", "outer", "head"), None, None),
            P(("inner", "outer"), "head", None),
            P(("inner", "outer"), "head", None),
        ),
        check_vma=False,
    )
```

profile of v0, /device:TPU:1, one launch (start us, length us, event | category | flops | bytes accessed | tf_op | source)
XLA Modules:
  0.0 186.2 jit_solution(12805209893710642443)
XLA Ops:
  0.6 0.0 copy-start.8
  0.6 0.0 copy-start.9
  0.7 1.9 %copy.78 = bf16[64,64,128]{2,0,1:T(8,128)(2,1)S(1)} copy(bf16[64,64,128]{2,1,0:T(8,128)(2,1)} %param.6) | data formatting | bytes 2097152 | tf_op args[0]
  2.6 1.9 %copy.79 = bf16[64,64,128]{2,0,1:T(8,128)(2,1)S(1)} copy(bf16[64,64,128]{2,1,0:T(8,128)(2,1)} %param.9) | data formatting | bytes 2097152 | tf_op args[3]
  4.5 1.7 pad_maximum_fusion
  6.2 14.0 %all-to-all-start = ((bf16[64,64,256]{2,0,1:T(8,128)(2,1)}), bf16[64,64,256]{2,0,1:T(8,128)(2,1)S(1)}, u32[]{:S(2)}, u32[]{:S(2)}) async-start(bf16[64,64,256]{2,0,1:T(8,128)(2,1)} %pad_maximum_fusion), calls=%async_computation | async-start | bytes 4194304 | tf_op jit(solution)/shard_map/all_to_all | solution.py:15
  20.2 0.0 copy-done.8
  20.3 1.3 collective-permute-start
  21.6 1.3 collective-permute-start.1
  22.9 0.0 copy-done.9
  22.9 5.3 %collective-permute-start.2 = (bf16[256,2,128]{2,0,1:T(8,128)(2,1)S(1)}, bf16[256,2,128]{2,0,1:T(8,128)(2,1)S(1)}, u32[]{:S(2)}, u32[]{:S(2)}) collective-permute-start(bf16[256,2,128]{2,0,1:T(8,128)(2,1)S(1)} %copy.83), channel_id=1, source_target_pairs={{0,8},{4,12},{8,16},{12,20},{16,24},{20,28},{24,32},{28,36},{32,40... | collective-permute-start | bytes 393224 | tf_op jit(solution)/shard_map/ppermute | solution.py:25
  28.2 4.2 %collective-permute-start.3 = (bf16[256,2,128]{2,0,1:T(8,128)(2,1)S(1)}, bf16[256,2,128]{2,0,1:T(8,128)(2,1)S(1)}, u32[]{:S(2)}, u32[]{:S(2)}) collective-permute-start(bf16[256,2,128]{2,0,1:T(8,128)(2,1)S(1)} %copy.83), channel_id=1, source_target_pairs={{0,4},{4,8},{8,12},{12,16},{16,20},{20,24},{24,28},{28,32},{32,36}... | collective-permute-start | bytes 393224 | tf_op jit(solution)/shard_map/ppermute | solution.py:25
  32.4 0.6 iota_add_fusion.1
  33.0 0.0 collective-permute-done
  33.0 0.0 collective-permute-done.1
  33.0 1.0 collective-permute-done.2
  34.0 3.0 %collective-permute-done.3 = bf16[256,2,128]{2,0,1:T(8,128)(2,1)S(1)} collective-permute-done((bf16[256,2,128]{2,0,1:T(8,128)(2,1)S(1)}, bf16[256,2,128]{2,0,1:T(8,128)(2,1)S(1)}, u32[]{:S(2)}, u32[]{:S(2)}) %collective-permute-start.3) | collective-permute-done | bytes 131104 | tf_op jit(solution)/shard_map/ppermute | solution.py:25
  37.1 0.8 maximum_bitcast_fusion.1
  37.8 18.3 %all-to-all-done = bf16[64,64,256]{2,0,1:T(8,128)(2,1)S(1)} async-done(((bf16[64,64,256]{2,0,1:T(8,128)(2,1)}), bf16[64,64,256]{2,0,1:T(8,128)(2,1)S(1)}, u32[]{:S(2)}, u32[]{:S(2)}) %all-to-all-start) | async-done | bytes 2097184 | tf_op jit(solution)/shard_map/all_to_all | solution.py:15
  56.2 1.2 copy.81
  57.4 0.4 slice_bitcast_fusion
  57.7 0.5 copy_bitcast_fusion
  58.3 82.2 %while.15 = (s32[]{:T(128)}, bf16[2,256,8,128]{1,3,2,0:T(8,128)(2,1)}, f32[2,768,128]{2,0,1:T(2,128)}, f32[2,768,128]{2,0,1:T(2,128)}, bf16[2,768,128]{2,1,0:T(8...) while((s32[]{:T(128)}, ...), condition=%wide.region_4.5_spmd.clone, body=%wide.region_0.4_spmd.clone.sunk | while | flops 2034465536 | bytes 100394088 | solution.py:68
  58.3 0.0 copy-start.1
  58.3 0.0 copy-start.3
  58.3 0.0 copy-start.5
  58.3 1.0 compare_and_fusion.2
  59.4 4.7 %fusion.96 = (f32[8,256]{1,0:T(8,128)S(1)}, f32[8,256,768]{1,2,0:T(8,128)}) fusion(pred[256,768]{0,1:T(8,128)(4,1)S(1)} %compare_and_fusion.2, bf16[2,256,8,128]{3,1,2,0:T(8,128)(2,1)S(1)} %get-tuple-element.222, s32[]{:T(128)} %get-tuple-element.204, bf16[2,768,128]{2,1,0:T(8,128)(2,1)S(1)} %get-tuple-element.221), kind=kOutput, calls=%fused_computation.68.clone.1 | convolution fusion | flops 408945408 | bytes 7218176 | tf_op jit(solution)/shard_map/while/body/eval_jaxpr/sub | solution.py:36
  64.1 3.9 %fusion.97 = (f32[8,256]{1,0:T(8,128)S(1)}, f32[768,256,8]{1,0,2:T(8,128)S(1)}) fusion(f32[8,256,768]{1,2,0:T(8,128)} %get-tuple-element.187, f32[8,256]{1,0:T(8,128)S(1)} %get-tuple-element.188, bf16[2,256,8,128]{3,1,2,0:T(8,128)(2,1)S(1)} %get-tuple-element.224, s32[]{:T(128)} %get-tuple-element.204, bf16[2,768,128]{2,1,0:T(8,128)(2,1)S(1)} %copy-done.7), kind=kOutput, calls=%fused_computation.4.clone.1 | convolution fusion | flops 407369728 | bytes 13321216 | tf_op jit(solution)/shard_map/while/body/eval_jaxpr/rgd,kd->grk/dot_general | solution.py:42
  68.1 0.6 copy-done
  68.7 1.2 fusion.98
  69.9 2.0 %fusion.100 = f32[768,128]{1,0:T(8,128)S(1)} fusion(bf16[8,256,768]{1,2,0:T(8,128)(2,1)S(1)} %fusion.98, bf16[2,256,8,128]{3,1,2,0:T(8,128)(2,1)} %copy-done.1, s32[]{:T(128)} %get-tuple-element.204), kind=kOutput, calls=%fused_computation.20.clone.1 | convolution fusion | flops 402751488 | bytes 4063744 | tf_op jit(solution)/shard_map/while/body/eval_jaxpr/grk,rgd->kd/dot_general | solution.py:50
  71.9 10.6 %dynamic_update_slice.19 = f32[2,768,128]{2,0,1:T(2,128)} dynamic-update-slice(f32[2,768,128]{2,0,1:T(2,128)} %get-tuple-element.206, f32[1,768,128]{2,0,1:T(1,128)S(1)} %bitcast.141, s32[]{:T(128)} %get-tuple-element.204, s32[]{:T(128)} %constant.21.clone.1..sunk, s32[]{:T(128)} %constant.21.clone.1..sunk) | dynamic-update-slice | bytes 786436 | tf_op jit(solution)/shard_map/while/body/jit(dynamic_update_index_in_dim)/dynamic_update_slice | solution.py:68
  82.5 2.3 %fusion.99 = bf16[2,256,8,128]{1,3,2,0:T(8,128)(2,1)} fusion(bf16[2,256,8,128]{1,3,2,0:T(8,128)(2,1)} %get-tuple-element.205, s32[]{:T(128)} %get-tuple-element.204, bf16[8,256,768]{1,2,0:T(8,128)(2,1)S(1)} %fusion.98, bf16[2,768,128]{2,1,0:T(8,128)(2,1)} %copy-done.3), kind=kOutput, calls=%fused_computation.18.clone.1 | convolution fusion | flops 402915328 | bytes 4391936 | tf_op jit(solution)/shard_map/while/body/eval_jaxpr/grk,kd->rgd/dot_general | solution.py:46
  84.8 4.0 %fusion.101 = f32[768,128,1]{1,0,2:T(8,128)S(1)} fusion(bf16[2,256,8,128]{3,1,2,0:T(8,128)(2,1)} %copy-done.5, s32[]{:T(128)} %get-tuple-element.204, f32[8,256,768]{1,2,0:T(8,128)} %get-tuple-element.187, f32[8,256]{1,0:T(8,128)S(1)} %get-tuple-element.188), kind=kOutput, calls=%fused_computation.10.clone.1 | convolution fusion | flops 405798912 | bytes 7217664 | tf_op jit(solution)/shard_map/while/body/eval_jaxpr/grk,rgd->kd/dot_general | solution.py:39
  88.8 10.6 %dynamic_update_slice.20 = f32[2,768,128]{2,0,1:T(2,128)} dynamic-update-slice(f32[2,768,128]{2,0,1:T(2,128)} %get-tuple-element.207, f32[1,768,128]{2,0,1:T(1,128)S(1)} %bitcast.142, s32[]{:T(128)} %get-tuple-element.204, s32[]{:T(128)} %constant.21.clone.1..sunk, s32[]{:T(128)} %constant.21.clone.1..sunk) | dynamic-update-slice | bytes 786436 | tf_op jit(solution)/shard_map/while/body/jit(dynamic_update_index_in_dim)/dynamic_update_slice | solution.py:68
  99.4 1.0 compare_and_fusion.2
  100.5 4.7 %fusion.96 = (f32[8,256]{1,0:T(8,128)S(1)}, f32[8,256,768]{1,2,0:T(8,128)}) fusion(pred[256,768]{0,1:T(8,128)(4,1)S(1)} %compare_and_fusion.2, bf16[2,256,8,128]{3,1,2,0:T(8,128)(2,1)S(1)} %get-tuple-element.222, s32[]{:T(128)} %get-tuple-element.204, bf16[2,768,128]{2,1,0:T(8,128)(2,1)S(1)} %get-tuple-element.221), kind=kOutput, calls=%fused_computation.68.clone.1 | convolution fusion | flops 408945408 | bytes 7218176 | tf_op jit(solution)/shard_map/while/body/eval_jaxpr/sub | solution.py:36
  105.2 0.0 copy-done.7
  105.2 3.9 %fusion.97 = (f32[8,256]{1,0:T(8,128)S(1)}, f32[768,256,8]{1,0,2:T(8,128)S(1)}) fusion(f32[8,256,768]{1,2,0:T(8,128)} %get-tuple-element.187, f32[8,256]{1,0:T(8,128)S(1)} %get-tuple-element.188, bf16[2,256,8,128]{3,1,2,0:T(8,128)(2,1)S(1)} %get-tuple-element.224, s32[]{:T(128)} %get-tuple-element.204, bf16[2,768,128]{2,1,0:T(8,128)(2,1)S(1)} %copy-done.7), kind=kOutput, calls=%fused_computation.4.clone.1 | convolution fusion | flops 407369728 | bytes 13321216 | tf_op jit(solution)/shard_map/while/body/eval_jaxpr/rgd,kd->grk/dot_general | solution.py:42
  109.2 0.6 copy-done
  109.8 1.2 fusion.98
  111.0 2.0 %fusion.100 = f32[768,128]{1,0:T(8,128)S(1)} fusion(bf16[8,256,768]{1,2,0:T(8,128)(2,1)S(1)} %fusion.98, bf16[2,256,8,128]{3,1,2,0:T(8,128)(2,1)} %copy-done.1, s32[]{:T(128)} %get-tuple-element.204), kind=kOutput, calls=%fused_computation.20.clone.1 | convolution fusion | flops 402751488 | bytes 4063744 | tf_op jit(solution)/shard_map/while/body/eval_jaxpr/grk,rgd->kd/dot_general | solution.py:50
  113.0 10.6 %dynamic_update_slice.19 = f32[2,768,128]{2,0,1:T(2,128)} dynamic-update-slice(f32[2,768,128]{2,0,1:T(2,128)} %get-tuple-element.206, f32[1,768,128]{2,0,1:T(1,128)S(1)} %bitcast.141, s32[]{:T(128)} %get-tuple-element.204, s32[]{:T(128)} %constant.21.clone.1..sunk, s32[]{:T(128)} %constant.21.clone.1..sunk) | dynamic-update-slice | bytes 786436 | tf_op jit(solution)/shard_map/while/body/jit(dynamic_update_index_in_dim)/dynamic_update_slice | solution.py:68
  123.6 2.3 %fusion.99 = bf16[2,256,8,128]{1,3,2,0:T(8,128)(2,1)} fusion(bf16[2,256,8,128]{1,3,2,0:T(8,128)(2,1)} %get-tuple-element.205, s32[]{:T(128)} %get-tuple-element.204, bf16[8,256,768]{1,2,0:T(8,128)(2,1)S(1)} %fusion.98, bf16[2,768,128]{2,1,0:T(8,128)(2,1)} %copy-done.3), kind=kOutput, calls=%fused_computation.18.clone.1 | convolution fusion | flops 402915328 | bytes 4391936 | tf_op jit(solution)/shard_map/while/body/eval_jaxpr/grk,kd->rgd/dot_general | solution.py:46
  125.9 4.0 %fusion.101 = f32[768,128,1]{1,0,2:T(8,128)S(1)} fusion(bf16[2,256,8,128]{3,1,2,0:T(8,128)(2,1)} %copy-done.5, s32[]{:T(128)} %get-tuple-element.204, f32[8,256,768]{1,2,0:T(8,128)} %get-tuple-element.187, f32[8,256]{1,0:T(8,128)S(1)} %get-tuple-element.188), kind=kOutput, calls=%fused_computation.10.clone.1 | convolution fusion | flops 405798912 | bytes 7217664 | tf_op jit(solution)/shard_map/while/body/eval_jaxpr/grk,rgd->kd/dot_general | solution.py:39
  129.9 10.6 %dynamic_update_slice.20 = f32[2,768,128]{2,0,1:T(2,128)} dynamic-update-slice(f32[2,768,128]{2,0,1:T(2,128)} %get-tuple-element.207, f32[1,768,128]{2,0,1:T(1,128)S(1)} %bitcast.142, s32[]{:T(128)} %get-tuple-element.204, s32[]{:T(128)} %constant.21.clone.1..sunk, s32[]{:T(128)} %constant.21.clone.1..sunk) | dynamic-update-slice | bytes 786436 | tf_op jit(solution)/shard_map/while/body/jit(dynamic_update_index_in_dim)/dynamic_update_slice | solution.py:68
  140.4 0.0 copy-done.4
  140.5 2.6 %copy.87 = bf16[256,2,8,128]{3,2,1,0:T(8,128)(2,1)} copy(bf16[256,2,8,128]{0,3,2,1:T(8,128)(2,1)} %bitcast.146) | data formatting | bytes 2097152 | tf_op jit(solution)/shard_map/convert_element_type | solution.py:97
  143.1 4.4 %all-to-all-start.1 = ((bf16[256,16,128]{2,1,0:T(8,128)(2,1)}), bf16[256,16,128]{2,1,0:T(8,128)(2,1)S(1)}, u32[]{:S(2)}, u32[]{:S(2)}) async-start(bf16[256,16,128]{2,1,0:T(8,128)(2,1)} %bitcast.11), calls=%async_computation.1 | async-start | bytes 2097152 | tf_op jit(solution)/shard_map/all_to_all | solution.py:96
  147.5 1.1 fusion.70
  148.6 1.3 collective-permute-start.6
  149.9 1.3 collective-permute-start.7
  151.2 1.1 fusion.71
  152.3 1.3 collective-permute-start.4
  153.6 1.3 collective-permute-start.5
  154.9 5.5 %collective-permute-done.6 = f32[256,2,128]{2,1,0:T(2,128)S(1)} collective-permute-done((f32[256,2,128]{2,1,0:T(2,128)S(1)}, f32[256,2,128]{2,1,0:T(2,128)S(1)}, u32[]{:S(2)}, u32[]{:S(2)}) %collective-permute-start.6) | collective-permute-done | bytes 262176 | tf_op jit(solution)/shard_map/ppermute | solution.py:25
  160.4 5.9 %collective-permute-done.7 = f32[256,2,128]{2,1,0:T(2,128)S(1)} collective-permute-done((f32[256,2,128]{2,1,0:T(2,128)S(1)}, f32[256,2,128]{2,1,0:T(2,128)S(1)}, u32[]{:S(2)}, u32[]{:S(2)}) %collective-permute-start.7) | collective-permute-done | bytes 262176 | tf_op jit(solution)/shard_map/ppermute | solution.py:25
  166.2 1.8 fusion.58
  168.0 1.5 collective-permute-done.4
  169.6 13.5 %collective-permute-done.5 = f32[256,2,128]{2,1,0:T(2,128)S(1)} collective-permute-done((f32[256,2,128]{2,1,0:T(2,128)S(1)}, f32[256,2,128]{2,1,0:T(2,128)S(1)}, u32[]{:S(2)}, u32[]{:S(2)}) %collective-permute-start.5) | collective-permute-done | bytes 262176 | tf_op jit(solution)/shard_map/ppermute | solution.py:25
  183.1 1.8 fusion.60
  184.9 0.0 all-to-all-done.1
  184.9 1.3 copy.88
  (33 shorter events, 0.1 us)
Async XLA Ops:
  0.6 19.6 %copy-start.8 = (bf16[256,2,128]{2,1,0:T(2,128)(2,1)S(1)}, bf16[256,2,128]{2,1,0:T(2,128)(2,1)}, u32[]{:S(2)}) copy-start(bf16[256,2,128]{2,1,0:T(2,128)(2,1)} %param.7) | copy-start | bytes 393220
  0.6 22.2 %copy-start.9 = (bf16[256,2,128]{2,1,0:T(2,128)(2,1)S(1)}, bf16[256,2,128]{2,1,0:T(2,128)(2,1)}, u32[]{:S(2)}) copy-start(bf16[256,2,128]{2,1,0:T(2,128)(2,1)} %param.8) | copy-start | bytes 393220
  6.2 50.0 %all-to-all-start = ((bf16[64,64,256]{2,0,1:T(8,128)(2,1)}), bf16[64,64,256]{2,0,1:T(8,128)(2,1)S(1)}, u32[]{:S(2)}, u32[]{:S(2)}) async-start(bf16[64,64,256]{2,0,1:T(8,128)(2,1)} %pad_maximum_fusion), calls=%async_computation | async-start | bytes 4194304 | tf_op jit(solution)/shard_map/all_to_all | solution.py:15
  20.3 12.7 %collective-permute-start = (bf16[256,2,128]{2,0,1:T(8,128)(2,1)S(1)}, bf16[256,2,128]{2,0,1:T(8,128)(2,1)S(1)}, u32[]{:S(2)}, u32[]{:S(2)}) collective-permute-start(bf16[256,2,128]{2,0,1:T(8,128)(2,1)S(1)} %copy.75), channel_id=1, source_target_pairs={{0,8},{4,12},{8,16},{12,20},{16,24},{20,28},{24,32},{28,36},{32,40... | collective-permute-start | bytes 393224 | tf_op jit(solution)/shard_map/ppermute | solution.py:25
  21.6 11.4 %collective-permute-start.1 = (bf16[256,2,128]{2,0,1:T(8,128)(2,1)S(1)}, bf16[256,2,128]{2,0,1:T(8,128)(2,1)S(1)}, u32[]{:S(2)}, u32[]{:S(2)}) collective-permute-start(bf16[256,2,128]{2,0,1:T(8,128)(2,1)S(1)} %copy.75), channel_id=1, source_target_pairs={{0,4},{4,8},{8,12},{12,16},{16,20},{20,24},{24,28},{28,32},{32,36}... | collective-permute-start | bytes 393224 | tf_op jit(solution)/shard_map/ppermute | solution.py:25
  22.9 11.1 %collective-permute-start.2 = (bf16[256,2,128]{2,0,1:T(8,128)(2,1)S(1)}, bf16[256,2,128]{2,0,1:T(8,128)(2,1)S(1)}, u32[]{:S(2)}, u32[]{:S(2)}) collective-permute-start(bf16[256,2,128]{2,0,1:T(8,128)(2,1)S(1)} %copy.83), channel_id=1, source_target_pairs={{0,8},{4,12},{8,16},{12,20},{16,24},{20,28},{24,32},{28,36},{32,40... | collective-permute-start | bytes 393224 | tf_op jit(solution)/shard_map/ppermute | solution.py:25
  28.2 8.9 %collective-permute-start.3 = (bf16[256,2,128]{2,0,1:T(8,128)(2,1)S(1)}, bf16[256,2,128]{2,0,1:T(8,128)(2,1)S(1)}, u32[]{:S(2)}, u32[]{:S(2)}) collective-permute-start(bf16[256,2,128]{2,0,1:T(8,128)(2,1)S(1)} %copy.83), channel_id=1, source_target_pairs={{0,4},{4,8},{8,12},{12,16},{16,20},{20,24},{24,28},{28,32},{32,36}... | collective-permute-start | bytes 393224 | tf_op jit(solution)/shard_map/ppermute | solution.py:25
  58.3 9.8 %copy-start.1 = (bf16[2,256,8,128]{3,1,2,0:T(8,128)(2,1)}, bf16[2,256,8,128]{3,1,2,0:T(8,128)(2,1)S(1)}, u32[]{:S(2)}) copy-start(bf16[2,256,8,128]{3,1,2,0:T(8,128)(2,1)S(1)} %get-tuple-element.222) | copy-start | bytes 3145732 | tf_op jit(solution)/shard_map/while
  58.3 9.8 %copy-start.3 = (bf16[2,768,128]{2,1,0:T(8,128)(2,1)}, bf16[2,768,128]{2,1,0:T(8,128)(2,1)S(1)}, u32[]{:S(2)}) copy-start(bf16[2,768,128]{2,1,0:T(8,128)(2,1)S(1)} %get-tuple-element.221) | copy-start | bytes 1179652 | tf_op jit(solution)/shard_map/while
  58.3 9.8 %copy-start.5 = (bf16[2,256,8,128]{3,1,2,0:T(8,128)(2,1)}, bf16[2,256,8,128]{3,1,2,0:T(8,128)(2,1)S(1)}, u32[]{:S(2)}) copy-start(bf16[2,256,8,128]{3,1,2,0:T(8,128)(2,1)S(1)} %get-tuple-element.224) | copy-start | bytes 3145732 | tf_op jit(solution)/shard_map/while
  58.3 5.8 %copy-start.7 = (bf16[2,768,128]{2,1,0:T(8,128)(2,1)S(1)}, bf16[2,768,128]{2,1,0:T(8,128)(2,1)}, u32[]{:S(2)}) copy-start(bf16[2,768,128]{2,1,0:T(8,128)(2,1)} %get-tuple-element.223) | copy-start | bytes 1179652 | tf_op jit(solution)/shard_map/while
  64.1 4.6 %copy-start = (f32[8,256,768]{1,2,0:T(8,128)S(1)}, f32[8,256,768]{1,2,0:T(8,128)}, u32[]{:S(2)}) copy-start(f32[8,256,768]{1,2,0:T(8,128)} %get-tuple-element.187) | copy-start | bytes 18874372 | tf_op jit(solution)/shard_map/while
  84.8 14.6 %copy-start.2 = (bf16[2,256,8,128]{3,1,2,0:T(8,128)(2,1)S(1)}, bf16[2,256,8,128]{3,1,2,0:T(8,128)(2,1)}, u32[]{:S(2)}) copy-start(bf16[2,256,8,128]{3,1,2,0:T(8,128)(2,1)} %copy-done.1) | copy-start | bytes 3145732 | tf_op jit(solution)/shard_map/while
  84.8 14.6 %copy-start.4 = (bf16[2,768,128]{2,1,0:T(8,128)(2,1)S(1)}, bf16[2,768,128]{2,1,0:T(8,128)(2,1)}, u32[]{:S(2)}) copy-start(bf16[2,768,128]{2,1,0:T(8,128)(2,1)} %copy-done.3) | copy-start | bytes 1179652 | tf_op jit(solution)/shard_map/while
  84.8 14.6 %copy-start.6 = (bf16[2,256,8,128]{3,1,2,0:T(8,128)(2,1)S(1)}, bf16[2,256,8,128]{3,1,2,0:T(8,128)(2,1)}, u32[]{:S(2)}) copy-start(bf16[2,256,8,128]{3,1,2,0:T(8,128)(2,1)} %copy-done.5) | copy-start | bytes 3145732 | tf_op jit(solution)/shard_map/while
  99.4 9.8 %copy-start.1 = (bf16[2,256,8,128]{3,1,2,0:T(8,128)(2,1)}, bf16[2,256,8,128]{3,1,2,0:T(8,128)(2,1)S(1)}, u32[]{:S(2)}) copy-start(bf16[2,256,8,128]{3,1,2,0:T(8,128)(2,1)S(1)} %get-tuple-element.222) | copy-start | bytes 3145732 | tf_op jit(solution)/shard_map/while
  99.4 9.8 %copy-start.3 = (bf16[2,768,128]{2,1,0:T(8,128)(2,1)}, bf16[2,768,128]{2,1,0:T(8,128)(2,1)S(1)}, u32[]{:S(2)}) copy-start(bf16[2,768,128]{2,1,0:T(8,128)(2,1)S(1)} %get-tuple-element.221) | copy-start | bytes 1179652 | tf_op jit(solution)/shard_map/while
  99.4 9.8 %copy-start.5 = (bf16[2,256,8,128]{3,1,2,0:T(8,128)(2,1)}, bf16[2,256,8,128]{3,1,2,0:T(8,128)(2,1)S(1)}, u32[]{:S(2)}) copy-start(bf16[2,256,8,128]{3,1,2,0:T(8,128)(2,1)S(1)} %get-tuple-element.224) | copy-start | bytes 3145732 | tf_op jit(solution)/shard_map/while
  99.4 5.8 %copy-start.7 = (bf16[2,768,128]{2,1,0:T(8,128)(2,1)S(1)}, bf16[2,768,128]{2,1,0:T(8,128)(2,1)}, u32[]{:S(2)}) copy-start(bf16[2,768,128]{2,1,0:T(8,128)(2,1)} %get-tuple-element.223) | copy-start | bytes 1179652 | tf_op jit(solution)/shard_map/while
  105.2 4.6 %copy-start = (f32[8,256,768]{1,2,0:T(8,128)S(1)}, f32[8,256,768]{1,2,0:T(8,128)}, u32[]{:S(2)}) copy-start(f32[8,256,768]{1,2,0:T(8,128)} %get-tuple-element.187) | copy-start | bytes 18874372 | tf_op jit(solution)/shard_map/while
  125.9 14.6 %copy-start.2 = (bf16[2,256,8,128]{3,1,2,0:T(8,128)(2,1)S(1)}, bf16[2,256,8,128]{3,1,2,0:T(8,128)(2,1)}, u32[]{:S(2)}) copy-start(bf16[2,256,8,128]{3,1,2,0:T(8,128)(2,1)} %copy-done.1) | copy-start | bytes 3145732 | tf_op jit(solution)/shard_map/while
  125.9 14.6 %copy-start.4 = (bf16[2,768,128]{2,1,0:T(8,128)(2,1)S(1)}, bf16[2,768,128]{2,1,0:T(8,128)(2,1)}, u32[]{:S(2)}) copy-start(bf16[2,768,128]{2,1,0:T(8,128)(2,1)} %copy-done.3) | copy-start | bytes 1179652 | tf_op jit(solution)/shard_map/while
  125.9 14.6 %copy-start.6 = (bf16[2,256,8,128]{3,1,2,0:T(8,128)(2,1)S(1)}, bf16[2,256,8,128]{3,1,2,0:T(8,128)(2,1)}, u32[]{:S(2)}) copy-start(bf16[2,256,8,128]{3,1,2,0:T(8,128)(2,1)} %copy-done.5) | copy-start | bytes 3145732 | tf_op jit(solution)/shard_map/while
  143.1 41.8 %all-to-all-start.1 = ((bf16[256,16,128]{2,1,0:T(8,128)(2,1)}), bf16[256,16,128]{2,1,0:T(8,128)(2,1)S(1)}, u32[]{:S(2)}, u32[]{:S(2)}) async-start(bf16[256,16,128]{2,1,0:T(8,128)(2,1)} %bitcast.11), calls=%async_computation.1 | async-start | bytes 2097152 | tf_op jit(solution)/shard_map/all_to_all | solution.py:96
  148.6 11.8 %collective-permute-start.6 = (f32[256,2,128]{2,1,0:T(2,128)S(1)}, f32[256,2,128]{2,1,0:T(2,128)S(1)}, u32[]{:S(2)}, u32[]{:S(2)}) collective-permute-start(f32[256,2,128]{2,1,0:T(2,128)S(1)} %get-tuple-element.110), channel_id=1, source_target_pairs={{4,0},{8,4},{12,8},{16,12},{20,16},{24,20},{28,24},{32,28},{36,32}... | collective-permute-start | bytes 786440 | tf_op jit(solution)/shard_map/ppermute | solution.py:25
  149.9 16.3 %collective-permute-start.7 = (f32[256,2,128]{2,1,0:T(2,128)S(1)}, f32[256,2,128]{2,1,0:T(2,128)S(1)}, u32[]{:S(2)}, u32[]{:S(2)}) collective-permute-start(f32[256,2,128]{2,1,0:T(2,128)S(1)} %get-tuple-element.111), channel_id=1, source_target_pairs={{8,0},{12,4},{16,8},{20,12},{24,16},{28,20},{32,24},{36,28},{40,32... | collective-permute-start | bytes 786440 | tf_op jit(solution)/shard_map/ppermute | solution.py:25
  152.3 17.3 %collective-permute-start.4 = (f32[256,2,128]{2,1,0:T(2,128)S(1)}, f32[256,2,128]{2,1,0:T(2,128)S(1)}, u32[]{:S(2)}, u32[]{:S(2)}) collective-permute-start(f32[256,2,128]{2,1,0:T(2,128)S(1)} %get-tuple-element.112), channel_id=1, source_target_pairs={{4,0},{8,4},{12,8},{16,12},{20,16},{24,20},{28,24},{32,28},{36,32}... | collective-permute-start | bytes 786440 | tf_op jit(solution)/shard_map/ppermute | solution.py:25
  153.6 29.5 %collective-permute-start.5 = (f32[256,2,128]{2,1,0:T(2,128)S(1)}, f32[256,2,128]{2,1,0:T(2,128)S(1)}, u32[]{:S(2)}, u32[]{:S(2)}) collective-permute-start(f32[256,2,128]{2,1,0:T(2,128)S(1)} %get-tuple-element.113), channel_id=1, source_target_pairs={{8,0},{12,4},{16,8},{20,12},{24,16},{28,20},{32,24},{36,28},{40,32... | collective-permute-start | bytes 786440 | tf_op jit(solution)/shard_map/ppermute | solution.py:25
where the time goes:
time: 189 us; the launch traced here: 186 us
  local copies, waits for them, and re-layouts  55.7 us (29%)
  waiting for transfers between devices  48.8 us (26%)
  starting transfers between devices  35.7 us (19%)
  matrix products  33.9 us (18%)
  other arithmetic  11.1 us (6%)
    dynamic_update_slice x4, local copies, waits for them, and re-layouts, block_grads(): lax.map(lambda packed: head_grads(packed[0], packed[1], packed[2], packed...  42.3 us
    ppermute x8, waiting for transfers between devices, from_behind(): return lax.ppermute(value, axis, pairs)  30.5 us
    all_to_all x1, waiting for transfers between devices, sent_together(): lax.all_to_all(both, axis, split_axis=split_dim, concat_axis=concat_dim,...  18.3 us
    ppermute x8, starting transfers between devices, from_behind(): return lax.ppermute(value, axis, pairs)  17.2 us
    all_to_all x1, starting transfers between devices, sent_together(): lax.all_to_all(both, axis, split_axis=split_dim, concat_axis=concat_dim,...  14 us
    sub x2, matrix products, head_grads(): probs = jnp.exp(scores - highest)  9.46 us
    dot_general x2, matrix products, head_grads(): jnp.einsum('grk,rgd->kd', probs_low, grad_part, preferred_element_type=jn...  7.95 us
    dot_general x2, matrix products, head_grads(): jnp.einsum('rgd,kd->grk', grad_part, value_part, preferred_element_type=j...  7.85 us
  transfers between devices with their start and end apart: 10, of which 7 were waited for; matrix products, arithmetic and copies ran while one was open for 4% of the time, Pallas kernels for 0%

commit v1 on v0

v1 whole, which is shorter than its diff:
```python
import functools

import jax
import jax.numpy as jnp
from jax import lax
from jax.experimental import pallas as pl
from jax.experimental.pallas import tpu as pltpu
from jax.sharding import PartitionSpec as P

MESH = pl.DeviceIdType.MESH
SCALE = 128**-0.5
LOG2E = 1.4426950408889634
MASKED = -1e30
ROWS = 512


def dot(a, b, a_dim, b_dim):
    return lax.dot_general(
        a, b, (((a_dim,), (b_dim,)), ((), ())), preferred_element_type=jnp.float32
    )


def unit_grads(kv, q_ref, g_ref, dq_ref, acc, s_ref, d_ref, first_token, far_off, near_off):
    offs = (far_off, near_off, None)
    tokens, heads, width = q_ref.shape
    per = ROWS // heads
    for i in range(tokens // per):
        part = pl.ds(i * per, per)
        q = q_ref[part].reshape(ROWS, width)
        g = g_ref[part].reshape(ROWS, width)
        highest = None
        for s in range(3):
            x = dot(kv[s][0][...], q, 1, 1)
            if s == 2:
                key = lax.broadcasted_iota(jnp.int32, x.shape, 0) * heads
                row = lax.broadcasted_iota(jnp.int32, x.shape, 1)
                x = jnp.where(key - row <= heads * first_token + i * ROWS, x, MASKED)
            s_ref[s] = x
            top = jnp.max(x, axis=0, keepdims=True)
            if offs[s] is not None:
                top = top - offs[s]
            highest = top if highest is None else jnp.maximum(highest, top)
        total = jnp.zeros((1, ROWS), jnp.float32)
        delta = jnp.zeros((1, ROWS), jnp.float32)
        for s in range(3):
            base = highest if offs[s] is None else highest + offs[s]
            e = jnp.exp2((s_ref[s] - base) * (SCALE * LOG2E))
            s_ref[s] = e
            total = total + jnp.sum(e, axis=0, keepdims=True)
            dp = dot(kv[s][1][...], g, 1, 1)
            d_ref[s] = dp
            delta = delta + jnp.sum(e * dp, axis=0, keepdims=True)
        inverse = 1.0 / total
        delta = delta * inverse
        dq = None
        for s in range(3):
            probs = s_ref[s] * inverse
            low = probs.astype(jnp.bfloat16)
            ds = (probs * (d_ref[s] - delta)).astype(jnp.bfloat16)
            dv = dot(low, g, 1, 0)
            dk = dot(ds, q, 1, 0) * SCALE
            if i == 0:
                acc[s][1][...] = dv
                acc[s][0][...] = dk
            else:
                acc[s][1][...] += dv
                acc[s][0][...] += dk
            term = dot(ds, kv[s][0][...], 0, 0)
            dq = term if dq is None else dq + term
        dq_ref[part] = (dq * SCALE).astype(jnp.bfloat16).reshape(per, heads, width)


def kernel(
    sizes,
    q_in, g_in, k_in, v_in,
    dq_out, dk_out, dv_out,
    kvb, qb, gb, dqb, acc, s_ref, d_ref, xs, xr, zs, zr,
    own_sem, kvown_sem, qg_send, qg_recv,
    z1_send, z1_recv, z0_send, z0_recv, x2_send, x2_recv, x_send, x_recv,
    dqown_sem, dq_send, dq_recv, xg_send, xg_recv, zg_send, zg_recv,
):
    n_inner, n_outer = sizes
    n_z = n_outer // 2
    blocks = n_inner * n_outer
    inner, outer, head = lax.axis_index("inner"), lax.axis_index("outer"), lax.axis_index("head")
    p, c = head // 2, head % 2
    z = outer % n_z
    block = inner * n_outer + outer
    turn_next = 1 - jnp.minimum(n_z - 1 - z, 1)
    turn_here = 1 - jnp.minimum(z, 1)
    turn_prev = 1 - jnp.minimum((z - 1) * (z - 1), 1)
    half = ((p + turn_here + turn_prev) % 2, (p + turn_here) % 2, p)

    def place(b, pp):
        return (b // n_outer, b % n_outer, pp * 2 + c)

    nxt = place((block + 1) % blocks, (p + turn_next) % 2)
    prv = place((block + blocks - 1) % blocks, (p + turn_here) % 2)
    beside = (inner, outer, (1 - p) * 2 + c)
    twin = (inner, outer, p * 2 + 1 - c)

    a = half[0]
    order = ((a, 0), (1 - a, 0), (1 - a, 1), (a, 1))

    def kv_head(u):
        h, j = order[u]
        return 4 * h + 2 * c + j

    def remote(src, dst, send, recv, device):
        return pltpu.make_async_remote_copy(
            src_ref=src, dst_ref=dst, send_sem=send, recv_sem=recv,
            device_id=device, device_id_type=MESH,
        )

    def own_copies(u):
        h, j = order[u]
        to = pl.ds(c * 64, 64)
        return [
            pltpu.make_async_copy(q_in.at[:, kv_head(u)], qb.at[h, j, to], own_sem.at[u, 0]),
            pltpu.make_async_copy(g_in.at[:, kv_head(u)], gb.at[h, j, to], own_sem.at[u, 1]),
        ]

    def kvown_copies(j):
        return [
            pltpu.make_async_copy(x.at[j], kvb.at[2, p, j, t], kvown_sem.at[j, t])
            for t, x in enumerate((k_in, v_in))
        ]

    def qg_copies(u):
        h, j = order[u]
        there = 4 * h + 2 * (1 - c) + j
        to = pl.ds(c * 64, 64)
        return [
            remote(q_in.at[:, there], qb.at[h, j, to], qg_send.at[u, 0], qg_recv.at[u, 0], twin),
            remote(g_in.at[:, there], gb.at[h, j, to], qg_send.at[u, 1], qg_recv.at[u, 1], twin),
        ]

    def z1_copies(j):
        return [
            remote(x.at[j], kvb.at[1, p, j, t], z1_send.at[j, t], z1_recv.at[j, t], nxt)
            for t, x in enumerate((k_in, v_in))
        ]

    def x2_copies(j):
        return [
            remote(x.at[j], kvb.at[2, p, j, t], x2_send.at[j, t], x2_recv.at[j, t], beside)
            for t, x in enumerate((k_in, v_in))
        ]

    def z0_copy(j):
        piece = kvb.at[1, half[1], j]
        return remote(piece, kvb.at[0, half[1], j], z0_send.at[j], z0_recv.at[j], nxt)

    def x_copy(s, j):
        piece = kvb.at[s, half[s], j]
        return remote(piece, piece, x_send.at[s, j], x_recv.at[s, j], beside)

    def xg_copy(s, j):
        return remote(xs.at[s, j], xr.at[s, j], xg_send.at[s, j], xg_recv.at[s, j], beside)

    def zg_copy(s, j):
        return remote(zs.at[s, j], zr.at[s, j], zg_send.at[s, j], zg_recv.at[s, j], prv)

    def dq_copies(u):
        h, j = order[u]
        at = kv_head(u)
        own = pltpu.make_async_copy(
            dqb.at[h, j, pl.ds(c * 64, 64)], dq_out.at[:, at], dqown_sem.at[u]
        )
        away = remote(
            dqb.at[h, j, pl.ds((1 - c) * 64, 64)], dq_out.at[:, at],
            dq_send.at[u], dq_recv.at[u], twin,
        )
        return own, away

    def start(copies):
        for copy in copies:
            copy.start()

    for u in range(4):
        start(own_copies(u))
    for j in range(2):
        start(kvown_copies(j))

    barrier = pltpu.get_barrier_semaphore()
    for peer in (twin, beside, nxt, prv):
        pl.semaphore_signal(barrier, inc=1, device_id=peer, device_id_type=MESH)
    pl.semaphore_wait(barrier, 4)

    start(z1_copies(0))
    start(x2_copies(0))
    start(qg_copies(0))
    start(qg_copies(1))

    def wait_x2(j):
        for copy in x2_copies(j):
            copy.wait_recv()

    for j in range(2):
        for copy in z1_copies(j):
            copy.wait_recv()
        z0_copy(j).start()
        x_copy(1, j).start()
        if j == 0:
            start(z1_copies(1))
            start(x2_copies(1))
            start(qg_copies(2))
            start(qg_copies(3))
    z0_copy(0).wait_recv()
    x_copy(0, 0).start()
    for j in range(2):
        for copy in kvown_copies(j):
            copy.wait()

    first_token = 128 * p
    far_off = (1 - jnp.minimum(block // 2, 1)).astype(jnp.float32) * (-MASKED)
    near_off = (1 - jnp.minimum(block, 1)).astype(jnp.float32) * (-MASKED)

    def export(s, j):
        h = 1 - half[s]
        for t in range(2):
            xs[s, j, t] = acc[s, h, j, t].astype(jnp.bfloat16)
        xg_copy(s, j).start()

    def compute(u):
        h, j = order[u]
        for copy in own_copies(u):
            copy.wait()
        for copy in qg_copies(u):
            copy.wait_recv()
        if u in (0, 3):
            @pl.when(half[1] != a)
            def _():
                x_copy(1, j).wait_recv()

            @pl.when(p != a)
            def _():
                wait_x2(j)
        else:
            x_copy(0, j).wait_recv()

            @pl.when(half[1] == a)
            def _():
                x_copy(1, j).wait_recv()

            @pl.when(p == a)
            def _():
                wait_x2(j)
        unit_grads(
            [(kvb.at[s, h, j, 0], kvb.at[s, h, j, 1]) for s in range(3)],
            qb.at[h, j], gb.at[h, j], dqb.at[h, j],
            [(acc.at[s, h, j, 0], acc.at[s, h, j, 1]) for s in range(3)],
            s_ref, d_ref, first_token, far_off, near_off,
        )
        start(dq_copies(u))

    def pass_on(s, j):
        xg_copy(s, j).wait_recv()
        if s == 1:
            zg_copy(0, j).wait_recv()
        for t in range(2):
            value = acc[s, half[s], j, t] + xr[s, j, t].astype(jnp.float32)
            if s == 1:
                value = value + zr[0, j, t].astype(jnp.float32)
            zs[s, j, t] = value.astype(jnp.bfloat16)
        zg_copy(s, j).start()

    def finish(j):
        xg_copy(2, j).wait_recv()
        zg_copy(1, j).wait_recv()
        for t, out in enumerate((dk_out, dv_out)):
            value = acc[2, p, j, t] + xr[2, j, t].astype(jnp.float32)
            out[j] = (value + zr[1, j, t].astype(jnp.float32)).astype(jnp.bfloat16)

    compute(0)
    z0_copy(1).wait_recv()
    x_copy(0, 1).start()
    compute(1)
    for s in range(3):
        export(s, 0)
    compute(2)
    export(0, 1)
    for s in (1, 2):
        pl.when(half[s] == a)(functools.partial(export, s, 1))
    pass_on(0, 0)
    compute(3)
    for s in (1, 2):
        pl.when(half[s] != a)(functools.partial(export, s, 1))
    pass_on(1, 0)
    pass_on(0, 1)
    finish(0)
    pass_on(1, 1)
    finish(1)

    for u in range(4):
        own, away = dq_copies(u)
        own.wait()
        away.wait_recv()
        away.wait_send()
        for copy in qg_copies(u):
            copy.wait_send()
    for j in range(2):
        for copy in z1_copies(j) + x2_copies(j):
            copy.wait_send()
        z0_copy(j).wait_send()
        for s in range(2):
            x_copy(s, j).wait_send()
            zg_copy(s, j).wait_send()
        for s in range(3):
            xg_copy(s, j).wait_send()


def shards(sizes, queries, key_rows, value_rows, grad_out):
    tokens, heads, width = queries.shape
    keys, groups, _ = key_rows.shape
    split = (tokens, 8, heads // 8, width)
    bf16, f32 = jnp.bfloat16, jnp.float32
    any_space = pl.BlockSpec(memory_space=pl.ANY)
    vmem = pl.BlockSpec(memory_space=pltpu.VMEM)
    dma = pltpu.SemaphoreType.DMA
    unit = (2, 2, 2 * tokens, heads // 8, width)
    dq, dk, dv = pl.pallas_call(
        functools.partial(kernel, sizes),
        out_shape=(
            jax.ShapeDtypeStruct(split, bf16),
            jax.ShapeDtypeStruct((groups, keys, width), bf16),
            jax.ShapeDtypeStruct((groups, keys, width), bf16),
        ),
        in_specs=[any_space] * 4,
        out_specs=(any_space, vmem, vmem),
        scratch_shapes=[
            pltpu.VMEM((3, 2, 2, 2, keys, width), bf16),
            pltpu.VMEM(unit, bf16),
            pltpu.VMEM(unit, bf16),
            pltpu.VMEM(unit, bf16),
            pltpu.VMEM((3, 2, 2, 2, keys, width), f32),
            pltpu.VMEM((3, keys, ROWS), f32),
            pltpu.VMEM((3, keys, ROWS), f32),
            pltpu.VMEM((3, 2, 2, keys, width), bf16),
            pltpu.VMEM((3, 2, 2, keys, width), bf16),
            pltpu.VMEM((2, 2, 2, keys, width), bf16),
            pltpu.VMEM((2, 2, 2, keys, width), bf16),
            dma((4, 2)), dma((2, 2)), dma((4, 2)), dma((4, 2)),
            dma((2, 2)), dma((2, 2)), dma((2,)), dma((2,)),
            dma((2, 2)), dma((2, 2)), dma((2, 2)), dma((2, 2)),
            dma((4,)), dma((4,)), dma((4,)),
            dma((3, 2)), dma((3, 2)), dma((2, 2)), dma((2, 2)),
        ],
        compiler_params=pltpu.CompilerParams(collective_id=0, has_side_effects=True),
        name="window_grads",
    )(
        queries.reshape(split), grad_out.reshape(split),
        key_rows.transpose(1, 0, 2), value_rows.transpose(1, 0, 2),
    )
    return dq.reshape(queries.shape), dk.transpose(1, 0, 2), dv.transpose(1, 0, 2)


def solution(mesh):
    rows = P(("inner", "outer", "head"), None, None)
    groups = P(("inner", "outer"), "head", None)
    return jax.shard_map(
        functools.partial(shards, (mesh.shape["inner"], mesh.shape["outer"])),
        mesh=mesh,
        in_specs=(rows, groups, groups, rows),
        out_specs=(rows, groups, groups),
        check_vma=False,
    )
```

time: 189 us -> 68.7 us (0.36)
  the two profiles are of different devices: /device:TPU:1 before, /device:TPU:2 now
where the time goes in v1:
time: 68.7 us; the launch traced here: 68.4 us
  Pallas kernels  61.3 us (89%)
  local copies, waits for them, and re-layouts  6.49 us (9%)
    pallas_call x1, Pallas kernels, shards(): pl.pallas_call(functools.partial(kernel, sizes), out_shape=(jax.ShapeDtyp...  61.3 us
    unnamed x5, local copies, waits for them, and re-layouts  4.79 us
    transpose x1, local copies, waits for them, and re-layouts, shards(): value_rows.transpose(1, 0, 2)  1.7 us

profile of v1, /device:TPU:2, one launch (start us, length us, event | category | flops | bytes accessed | tf_op | source)
XLA Modules:
  0.0 68.4 jit_solution(529570966435467664)
XLA Ops:
  0.6 1.7 %copy_bitcast_fusion = (bf16[2,256,128]{2,1,0:T(8,128)(2,1)}, bf16[2,256,128]{2,1,0:T(8,128)(2,1)}) fusion(bf16[256,2,128]{2,1,0:T(2,128)(2,1)} %param.6, bf16[256,2,128]{2,1,0:T(2,128)(2,1)} %param.5), kind=kLoop, calls=%fused_computation | loop fusion | bytes 524288 | tf_op jit(solution)/shard_map/transpose | solution.py:353
  2.3 61.3 %window_grads.1 = (bf16[64,8,8,128]{3,2,1,0:T(8,128)(2,1)}, bf16[2,256,128]{2,1,0:T(8,128)(2,1)}, bf16[2,256,128]{2,1,0:T(8,128)(2,1)}) custom-call(bf16[64,8,8,128]{3,2,1,0:T(8,128)(2,1)} %bitcast.9, bf16[64,8,8,128]{3,2,1,0:T(8,128)(2,1)} %bitcast.10, bf16[2,256,128]{2,1,0:T(8,128)(2,1)} %get-tuple-element.13.k_in, bf16[2,256,128]{2,1,0:T(8,128)(2,1)} %get-tuple-element.12.v_in), custom_call_target="tpu_custom_call" | custom-call | tf_op jit(solution)/shard_map/window_grads/pallas_call | solution.py:322
  63.7 0.0 copy-start
  63.7 1.7 %copy.9 = bf16[256,2,128]{2,1,0:T(2,128)(2,1)} copy(bf16[256,2,128]{2,0,1:T(8,128)(2,1)} %bitcast.13) | data formatting | bytes 262144
  65.4 0.0 copy-done
  65.4 0.8 %copy.10 = bf16[256,2,128]{2,1,0:T(2,128)(2,1)} copy(bf16[256,2,128]{2,0,1:T(8,128)(2,1)S(1)} %bitcast.12) | data formatting | bytes 262144
  66.2 2.3 %copy.14 = bf16[64,64,128]{2,1,0:T(8,128)(2,1)} copy(bf16[64,64,128]{2,1,0:T(8,128)(2,1)} %bitcast.11) | data formatting | bytes 2097152
Async XLA Ops:
  63.7 1.7 %copy-start = (bf16[2,256,128]{2,1,0:T(8,128)(2,1)S(1)}, bf16[2,256,128]{2,1,0:T(8,128)(2,1)}, u32[]{:S(2)}) copy-start(bf16[2,256,128]{2,1,0:T(8,128)(2,1)} %get-tuple-element.8) | copy-start | bytes 393220

commit v2 on v1

v2 whole, which is shorter than its diff:
```python
import functools

import jax
import jax.numpy as jnp
from jax import lax
from jax.experimental import pallas as pl
from jax.experimental.pallas import tpu as pltpu
from jax.sharding import PartitionSpec as P

MESH = pl.DeviceIdType.MESH
SCALE = 128**-0.5
LOG2E = 1.4426950408889634
MASKED = -1e30
ROWS = 512


def dot(a, b, a_dim, b_dim):
    return lax.dot_general(
        a, b, (((a_dim,), (b_dim,)), ((), ())), preferred_element_type=jnp.float32
    )


def unit_grads(kv, q_ref, g_ref, dq_ref, acc, s_ref, d_ref, first_token, far_off, near_off, between):
    offs = (far_off, near_off, None)
    tokens, heads, width = q_ref.shape
    per = ROWS // heads
    for i in range(tokens // per):
        if i:
            between()
        part = pl.ds(i * per, per)
        q = q_ref[part].reshape(ROWS, width)
        g = g_ref[part].reshape(ROWS, width)
        highest = None
        for s in range(3):
            x = dot(kv[s][0][...], q, 1, 1)
            if s == 2:
                key = lax.broadcasted_iota(jnp.int32, x.shape, 0) * heads
                row = lax.broadcasted_iota(jnp.int32, x.shape, 1)
                x = jnp.where(key - row <= heads * first_token + i * ROWS, x, MASKED)
            s_ref[s] = x
            top = jnp.max(x, axis=0, keepdims=True)
            if offs[s] is not None:
                top = top - offs[s]
            highest = top if highest is None else jnp.maximum(highest, top)
        total = jnp.zeros((1, ROWS), jnp.float32)
        delta = jnp.zeros((1, ROWS), jnp.float32)
        for s in range(3):
            base = highest if offs[s] is None else highest + offs[s]
            e = jnp.exp2((s_ref[s] - base) * (SCALE * LOG2E))
            s_ref[s] = e
            total = total + jnp.sum(e, axis=0, keepdims=True)
            dp = dot(kv[s][1][...], g, 1, 1)
            d_ref[s] = dp
            delta = delta + jnp.sum(e * dp, axis=0, keepdims=True)
        inverse = 1.0 / total
        delta = delta * inverse
        dq = None
        for s in range(3):
            probs = s_ref[s] * inverse
            low = probs.astype(jnp.bfloat16)
            ds = (probs * (d_ref[s] - delta)).astype(jnp.bfloat16)
            dv = dot(low, g, 1, 0)
            dk = dot(ds, q, 1, 0) * SCALE
            if i == 0:
                acc[s][1][...] = dv
                acc[s][0][...] = dk
            else:
                acc[s][1][...] += dv
                acc[s][0][...] += dk
            term = dot(ds, kv[s][0][...], 0, 0)
            dq = term if dq is None else dq + term
        dq_ref[part] = (dq * SCALE).astype(jnp.bfloat16).reshape(per, heads, width)


def kernel(
    sizes,
    q_in, g_in, k_in, v_in,
    dq_out, dk_out, dv_out,
    kvb, qb, gb, dqb, acc, s_ref, d_ref, raw, wide,
    far_s, far_r, near_s, near_r, xs, xr,
    raw_sem, own_sem, qg_send, qg_recv,
    near_kv_send, near_kv_recv, far_kv_send, far_kv_recv, x_kv_send, x_kv_recv,
    dqown_sem, dq_send, dq_recv,
    far_send, far_recv, near_send, near_recv, x_send, x_recv,
):
    n_inner, n_outer = sizes
    n_z = n_outer // 2
    blocks = n_inner * n_outer
    inner, outer, head = lax.axis_index("inner"), lax.axis_index("outer"), lax.axis_index("head")
    p, c = head // 2, head % 2
    z = outer % n_z
    block = inner * n_outer + outer
    turn_next = 1 - jnp.minimum(n_z - 1 - z, 1)
    turn_here = 1 - jnp.minimum(z, 1)
    turn_prev = 1 - jnp.minimum((z - 1) * (z - 1), 1)
    a = (p + turn_here + turn_prev) % 2
    h1 = (p + turn_here) % 2

    def place(b, pp):
        return (b // n_outer, b % n_outer, pp * 2 + c)

    nxt = place((block + 1) % blocks, (p + turn_next) % 2)
    prv = place((block + blocks - 1) % blocks, (p + turn_here) % 2)
    beside = (inner, outer, (1 - p) * 2 + c)
    twin = (inner, outer, p * 2 + 1 - c)
    order = ((a, 0), (1 - a, 0), (a, 1), (1 - a, 1))

    def kv_head(u):
        h, j = order[u]
        return 4 * h + 2 * c + j

    def remote(src, dst, send, recv, device):
        return pltpu.make_async_remote_copy(
            src_ref=src, dst_ref=dst, send_sem=send, recv_sem=recv,
            device_id=device, device_id_type=MESH,
        )

    def own_copies(u):
        h, j = order[u]
        to = pl.ds(c * 64, 64)
        return [
            pltpu.make_async_copy(q_in.at[:, kv_head(u)], qb.at[h, j, to], own_sem.at[u, 0]),
            pltpu.make_async_copy(g_in.at[:, kv_head(u)], gb.at[h, j, to], own_sem.at[u, 1]),
        ]

    def qg_copies(u):
        h, j = order[u]
        there = 4 * h + 2 * (1 - c) + j
        to = pl.ds(c * 64, 64)
        return [
            remote(q_in.at[:, there], qb.at[h, j, to], qg_send.at[u, 0], qg_recv.at[u, 0], twin),
            remote(g_in.at[:, there], gb.at[h, j, to], qg_send.at[u, 1], qg_recv.at[u, 1], twin),
        ]

    def near_kv(j, t):
        return remote(
            kvb.at[2, p, j, t], kvb.at[1, p, j, t],
            near_kv_send.at[j, t], near_kv_recv.at[j, t], nxt,
        )

    def far_kv(h, j, t):
        return remote(
            kvb.at[1, h, j, t], kvb.at[0, h, j, t],
            far_kv_send.at[h, j, t], far_kv_recv.at[h, j, t], nxt,
        )

    def x_kv(s, j, t):
        piece = kvb.at[s, p if s == 2 else h1, j, t]
        return remote(piece, piece, x_kv_send.at[s - 1, j, t], x_kv_recv.at[s - 1, j, t], beside)

    def far_grad(h, j, t):
        return remote(
            far_s.at[h, j, t], far_r.at[h, j, t],
            far_send.at[h, j, t], far_recv.at[h, j, t], prv,
        )

    def near_grad(j, t):
        return remote(
            near_s.at[j, t], near_r.at[j, t], near_send.at[j, t], near_recv.at[j, t], prv
        )

    def x_grad(s, j, t):
        return remote(
            xs.at[s - 1, j, t], xr.at[s - 1, j, t],
            x_send.at[s - 1, j, t], x_recv.at[s - 1, j, t], beside,
        )

    def dq_copies(u):
        h, j = order[u]
        at = kv_head(u)
        own = pltpu.make_async_copy(
            dqb.at[h, j, pl.ds(c * 64, 64)], dq_out.at[:, at], dqown_sem.at[u]
        )
        away = remote(
            dqb.at[h, j, pl.ds((1 - c) * 64, 64)], dq_out.at[:, at],
            dq_send.at[u], dq_recv.at[u], twin,
        )
        return own, away

    def start(copies):
        for copy in copies:
            copy.start()

    raw_copies = [
        pltpu.make_async_copy(x, raw.at[t], raw_sem.at[t]) for t, x in enumerate((k_in, v_in))
    ]
    start(raw_copies)
    barrier = pltpu.get_barrier_semaphore()
    for peer in (twin, beside, nxt, prv):
        pl.semaphore_signal(barrier, inc=1, device_id=peer, device_id_type=MESH)
    for u in range(4):
        start(own_copies(u))
    keys = kvb.shape[4]
    for t in range(2):
        raw_copies[t].wait()
        wide[t] = raw[t].astype(jnp.float32)
        for j in range(2):
            kvb[2, p, j, t] = wide[t, pl.ds(j, keys, stride=2)].astype(jnp.bfloat16)
    pl.semaphore_wait(barrier, 4)

    for t in range(2):
        near_kv(0, t).start()
        x_kv(2, 0, t).start()
    start(qg_copies(0))
    start(qg_copies(1))

    def relay_near(j):
        for t in range(2):
            near_kv(j, t).wait_recv()
            far_kv(h1, j, t).start()
            x_kv(1, j, t).start()

    def relay_far(j):
        for t in range(2):
            x_kv(1, j, t).wait_recv()
            far_kv(1 - h1, j, t).start()

    relay_near(0)
    for t in range(2):
        near_kv(1, t).start()
        x_kv(2, 1, t).start()
    start(qg_copies(2))
    start(qg_copies(3))
    relay_far(0)

    first_token = 128 * p
    far_off = (1 - jnp.minimum(block // 2, 1)).astype(jnp.float32) * (-MASKED)
    near_off = (1 - jnp.minimum(block, 1)).astype(jnp.float32) * (-MASKED)

    def compute(u, between):
        h, j = order[u]
        for copy in own_copies(u):
            copy.wait()
        for copy in qg_copies(u):
            copy.wait_recv()
        for t in range(2):
            far_kv(h, j, t).wait_recv()
            if u in (0, 2):
                x_kv(2, j, t).wait_recv()
        unit_grads(
            [(kvb.at[s, h, j, 0], kvb.at[s, h, j, 1]) for s in range(3)],
            qb.at[h, j], gb.at[h, j], dqb.at[h, j],
            [(acc.at[s, h, j, 0], acc.at[s, h, j, 1]) for s in range(3)],
            s_ref, d_ref, first_token, far_off, near_off, between,
        )
        for t in range(2):
            far_s[h, j, t] = acc[0, h, j, t].astype(jnp.bfloat16)
            far_grad(h, j, t).start()
        start(dq_copies(u))

    def send_last(j):
        for t in range(2):
            xs[1, j, t] = acc[2, 1 - p, j, t].astype(jnp.bfloat16)
            x_grad(2, j, t).start()

    def send_middle(j):
        for t in range(2):
            far_grad(1 - h1, j, t).wait_recv()
            value = acc[1, 1 - h1, j, t] + far_r[1 - h1, j, t].astype(jnp.float32)
            xs[0, j, t] = value.astype(jnp.bfloat16)
            x_grad(1, j, t).start()

    def pass_on(j):
        for t in range(2):
            far_grad(h1, j, t).wait_recv()
            x_grad(1, j, t).wait_recv()
            value = acc[1, h1, j, t] + far_r[h1, j, t].astype(jnp.float32)
            value = value + xr[0, j, t].astype(jnp.float32)
            near_s[j, t] = value.astype(jnp.bfloat16)
            near_grad(j, t).start()

    def finish(j):
        for t in range(2):
            x_grad(2, j, t).wait_recv()
            near_grad(j, t).wait_recv()
            value = acc[2, p, j, t] + xr[1, j, t].astype(jnp.float32)
            value = value + near_r[j, t].astype(jnp.float32)
            wide[t, pl.ds(j, keys, stride=2)] = value

    def nothing():
        pass

    compute(0, functools.partial(relay_near, 1))
    compute(1, functools.partial(relay_far, 1))
    send_last(0)
    compute(2, nothing)
    compute(3, functools.partial(send_middle, 0))
    send_last(1)
    pass_on(0)
    send_middle(1)
    pass_on(1)
    finish(0)
    finish(1)
    dk_out[...] = wide[0].astype(jnp.bfloat16)
    dv_out[...] = wide[1].astype(jnp.bfloat16)

    for u in range(4):
        own, away = dq_copies(u)
        own.wait()
        away.wait_recv()
        away.wait_send()
        for copy in qg_copies(u):
            copy.wait_send()
    for j in range(2):
        for t in range(2):
            near_kv(j, t).wait_send()
            near_grad(j, t).wait_send()
            for s in (1, 2):
                x_kv(s, j, t).wait_send()
                x_grad(s, j, t).wait_send()
            for h in range(2):
                far_kv(h, j, t).wait_send()
                far_grad(h, j, t).wait_send()


def shards(sizes, queries, key_rows, value_rows, grad_out):
    tokens, heads, width = queries.shape
    keys, groups, _ = key_rows.shape
    split = (tokens, 8, heads // 8, width)
    bf16, f32 = jnp.bfloat16, jnp.float32
    any_space = pl.BlockSpec(memory_space=pl.ANY)
    vmem = pl.BlockSpec(memory_space=pltpu.VMEM)
    dma = pltpu.SemaphoreType.DMA
    unit = (2, 2, 2 * tokens, heads // 8, width)
    pieces = (2, 2, keys, width)
    eight, four = dma((2, 2, 2)), dma((2, 2))
    flat = (groups * keys, width)
    dq, dk, dv = pl.pallas_call(
        functools.partial(kernel, sizes),
        out_shape=(
            jax.ShapeDtypeStruct(split, bf16),
            jax.ShapeDtypeStruct(flat, bf16),
            jax.ShapeDtypeStruct(flat, bf16),
        ),
        in_specs=[any_space] * 4,
        out_specs=(any_space, vmem, vmem),
        scratch_shapes=[
            pltpu.VMEM((3, 2) + pieces, bf16),
            pltpu.VMEM(unit, bf16),
            pltpu.VMEM(unit, bf16),
            pltpu.VMEM(unit, bf16),
            pltpu.VMEM((3, 2) + pieces, f32),
            pltpu.VMEM((3, keys, ROWS), f32),
            pltpu.VMEM((3, keys, ROWS), f32),
            pltpu.VMEM((2,) + flat, bf16),
            pltpu.VMEM((2,) + flat, f32),
            pltpu.VMEM((2,) + pieces, bf16),
            pltpu.VMEM((2,) + pieces, bf16),
            pltpu.VMEM(pieces, bf16),
            pltpu.VMEM(pieces, bf16),
            pltpu.VMEM((2,) + pieces, bf16),
            pltpu.VMEM((2,) + pieces, bf16),
            dma((2,)), dma((4, 2)), dma((4, 2)), dma((4, 2)),
            four, four, eight, eight, eight, eight,
            dma((4,)), dma((4,)), dma((4,)),
            eight, eight, four, four, eight, eight,
        ],
        compiler_params=pltpu.CompilerParams(collective_id=0, has_side_effects=True),
        name="window_grads",
    )(
        queries.reshape(split), grad_out.reshape(split),
        key_rows.reshape(flat), value_rows.reshape(flat),
    )
    return dq.reshape(queries.shape), dk.reshape(key_rows.shape), dv.reshape(key_rows.shape)


def solution(mesh):
    rows = P(("inner", "outer", "head"), None, None)
    groups = P(("inner", "outer"), "head", None)
    return jax.shard_map(
        functools.partial(shards, (mesh.shape["inner"], mesh.shape["outer"])),
        mesh=mesh,
        in_specs=(rows, groups, groups, rows),
        out_specs=(rows, groups, groups),
        check_vma=False,
    )
```

time: 68.7 us -> 59.9 us (0.87)
  Pallas kernels: 61.3 us -> 55.2 us
  local copies, waits for them, and re-layouts: 6.49 us -> 3.91 us
    pallas_call x1, Pallas kernels: 61.3 us -> 55.2 us  [shards(): pl.pallas_call(functools.partial(kernel, sizes), out_shape=(jax.ShapeDtyp...]
    transpose x1 -> x0, local copies, waits for them, and re-layouts: 1.7 us -> none  [shards(): value_rows.transpose(1, 0, 2)]
    unnamed x5 -> x7, local copies, waits for them, and re-layouts: 4.79 us -> 3.91 us
where the time goes in v2:
time: 59.9 us; the launch traced here: 59.7 us
  Pallas kernels  55.2 us (92%)
  local copies, waits for them, and re-layouts  3.91 us (7%)
  between operations  0.65 us (1%)
    pallas_call x1, Pallas kernels, shards(): pl.pallas_call(functools.partial(kernel, sizes), out_shape=(jax.ShapeDtyp...  55.2 us
    unnamed x7, local copies, waits for them, and re-layouts  3.91 us

profile of v2, /device:TPU:2, one launch (start us, length us, event | category | flops | bytes accessed | tf_op | source)
XLA Modules:
  0.0 59.7 jit_solution(13293988669046699819)
XLA Ops:
  0.6 55.2 %window_grads.1 = (bf16[64,8,8,128]{3,2,1,0:T(8,128)(2,1)}, bf16[512,128]{1,0:T(8,128)(2,1)}, bf16[512,128]{1,0:T(8,128)(2,1)}) custom-call(bf16[64,8,8,128]{3,2,1,0:T(8,128)(2,1)} %bitcast.7, bf16[64,8,8,128]{3,2,1,0:T(8,128)(2,1)} %bitcast.8, bf16[512,128]{1,0:T(8,128)(2,1)} %bitcast.10, bf16[512,128]{1,0:T(8,128)(2,1)} %bitcast.11), custom_call_target="tpu_custom_call" | custom-call | tf_op jit(solution)/shard_map/window_grads/pallas_call | solution.py:328
  55.8 0.0 copy-start.1
  55.8 2.3 %copy.10 = bf16[64,64,128]{2,1,0:T(8,128)(2,1)} copy(bf16[64,64,128]{2,1,0:T(8,128)(2,1)} %bitcast.9) | data formatting | bytes 2097152
  58.1 0.0 copy-done.1
  58.1 0.0 copy-start
  58.1 0.7 %copy.11 = bf16[256,2,128]{2,1,0:T(2,128)(2,1)} copy(bf16[256,2,128]{2,1,0:T(2,128)(2,1)S(1)} %bitcast.13) | data formatting | bytes 262144
  58.8 0.3 copy-done
  59.1 0.7 %copy.12 = bf16[256,2,128]{2,1,0:T(2,128)(2,1)} copy(bf16[256,2,128]{2,1,0:T(2,128)(2,1)S(1)} %bitcast.12) | data formatting | bytes 262144
Async XLA Ops:
  55.8 2.3 %copy-start.1 = (bf16[512,128]{1,0:T(8,128)(2,1)S(1)}, bf16[512,128]{1,0:T(8,128)(2,1)}, u32[]{:S(2)}) copy-start(bf16[512,128]{1,0:T(8,128)(2,1)} %get-tuple-element.7) | copy-start | bytes 393220
  58.1 1.0 %copy-start = (bf16[512,128]{1,0:T(8,128)(2,1)S(1)}, bf16[512,128]{1,0:T(8,128)(2,1)}, u32[]{:S(2)}) copy-start(bf16[512,128]{1,0:T(8,128)(2,1)} %get-tuple-element.8) | copy-start | bytes 393220

commit v3 on v2

--- a/solution.py
+++ b/solution.py
@@ -14,13 +14,20 @@
 ROWS = 512
 
 
+PIECES = 4
+
+
 def dot(a, b, a_dim, b_dim):
     return lax.dot_general(
         a, b, (((a_dim,), (b_dim,)), ((), ())), preferred_element_type=jnp.float32
     )
 
 
-def unit_grads(kv, q_ref, g_ref, dq_ref, acc, s_ref, d_ref, first_token, far_off, near_off, between):
+def rows_of(ref):
+    return ref[...].reshape(-1, ref.shape[-1])
+
+
+def unit_grads(kv, q_ref, g_ref, dq_ref, acc, s_ref, d_ref, first_token, far_off, near_off, between, first_done):
     offs = (far_off, near_off, None)
     tokens, heads, width = q_ref.shape
     per = ROWS // heads
@@ -32,7 +39,7 @@
         g = g_ref[part].reshape(ROWS, width)
         highest = None
         for s in range(3):
-            x = dot(kv[s][0][...], q, 1, 1)
+            x = dot(rows_of(kv[s][0]), q, 1, 1)
             if s == 2:
                 key = lax.broadcasted_iota(jnp.int32, x.shape, 0) * heads
                 row = lax.broadcasted_iota(jnp.int32, x.shape, 1)
@@ -49,7 +56,7 @@
             e = jnp.exp2((s_ref[s] - base) * (SCALE * LOG2E))
             s_ref[s] = e
             total = total + jnp.sum(e, axis=0, keepdims=True)
-            dp = dot(kv[s][1][...], g, 1, 1)
+            dp = dot(rows_of(kv[s][1]), g, 1, 1)
             d_ref[s] = dp
             delta = delta + jnp.sum(e * dp, axis=0, keepdims=True)
         inverse = 1.0 / total
@@ -67,7 +74,9 @@
             else:
                 acc[s][1][...] += dv
                 acc[s][0][...] += dk
-            term = dot(ds, kv[s][0][...], 0, 0)
+            if s == 0 and i == tokens // per - 1:
+                first_done()
+            term = dot(ds, rows_of(kv[s][0]), 0, 0)
             dq = term if dq is None else dq + term
         dq_ref[part] = (dq * SCALE).astype(jnp.bfloat16).reshape(per, heads, width)
 
@@ -132,37 +141,37 @@
             remote(g_in.at[:, there], gb.at[h, j, to], qg_send.at[u, 1], qg_recv.at[u, 1], twin),
         ]
 
-    def near_kv(j, t):
+    def near_kv(j, i):
         return remote(
-            kvb.at[2, p, j, t], kvb.at[1, p, j, t],
-            near_kv_send.at[j, t], near_kv_recv.at[j, t], nxt,
-        )
-
-    def far_kv(h, j, t):
+            kvb.at[2, p, j, i], kvb.at[1, p, j, i],
+            near_kv_send.at[j, i], near_kv_recv.at[j, i], nxt,
+        )
+
+    def far_kv(h, j, i):
         return remote(
-            kvb.at[1, h, j, t], kvb.at[0, h, j, t],
-            far_kv_send.at[h, j, t], far_kv_recv.at[h, j, t], nxt,
-        )
-
-    def x_kv(s, j, t):
-        piece = kvb.at[s, p if s == 2 else h1, j, t]
-        return remote(piece, piece, x_kv_send.at[s - 1, j, t], x_kv_recv.at[s - 1, j, t], beside)
-
-    def far_grad(h, j, t):
+            kvb.at[1, h, j, i], kvb.at[0, h, j, i],
+            far_kv_send.at[h, j, i], far_kv_recv.at[h, j, i], nxt,
+        )
+
+    def x_kv(s, j, i):
+        piece = kvb.at[s, p if s == 2 else h1, j, i]
+        return remote(piece, piece, x_kv_send.at[s - 1, j, i], x_kv_recv.at[s - 1, j, i], beside)
+
+    def far_grad(h, j, i):
         return remote(
-            far_s.at[h, j, t], far_r.at[h, j, t],
-            far_send.at[h, j, t], far_recv.at[h, j, t], prv,
-        )
-
-    def near_grad(j, t):
+            far_s.at[h, j, i], far_r.at[h, j, i],
+            far_send.at[h, j, i], far_recv.at[h, j, i], prv,
+        )
+
+    def near_grad(j, i):
         return remote(
-            near_s.at[j, t], near_r.at[j, t], near_send.at[j, t], near_recv.at[j, t], prv
-        )
-
-    def x_grad(s, j, t):
+            near_s.at[j, i], near_r.at[j, i], near_send.at[j, i], near_recv.at[j, i], prv
+        )
+
+    def x_grad(s, j, i):
         return remote(
-            xs.at[s - 1, j, t], xr.at[s - 1, j, t],
-            x_send.at[s - 1, j, t], x_recv.at[s - 1, j, t], beside,
+            xs.at[s - 1, j, i], xr.at[s - 1, j, i],
+            x_send.at[s - 1, j, i], x_recv.at[s - 1, j, i], beside,
         )
 
     def dq_copies(u):
@@ -190,35 +199,43 @@
         pl.semaphore_signal(barrier, inc=1, device_id=peer, device_id_type=MESH)
     for u in range(4):
         start(own_copies(u))
-    keys = kvb.shape[4]
+    size = kvb.shape[4]
+
+    def at(i):
+        return i // 2, pl.ds(i % 2 * size, size)
+
+    def alternate(i, j):
+        return i // 2, pl.ds(i % 2 * 2 * size + j, size, stride=2)
+
     for t in range(2):
         raw_copies[t].wait()
         wide[t] = raw[t].astype(jnp.float32)
-        for j in range(2):
-            kvb[2, p, j, t] = wide[t, pl.ds(j, keys, stride=2)].astype(jnp.bfloat16)
+    for j in range(2):
+        for i in range(PIECES):
+            kvb[2, p, j, i] = wide[alternate(i, j)].astype(jnp.bfloat16)
     pl.semaphore_wait(barrier, 4)
 
-    for t in range(2):
-        near_kv(0, t).start()
-        x_kv(2, 0, t).start()
+    for i in range(PIECES):
+        near_kv(0, i).start()
+        x_kv(2, 0, i).start()
     start(qg_copies(0))
     start(qg_copies(1))
 
     def relay_near(j):
-        for t in range(2):
-            near_kv(j, t).wait_recv()
-            far_kv(h1, j, t).start()
-            x_kv(1, j, t).start()
+        for i in range(PIECES):
+            near_kv(j, i).wait_recv()
+            far_kv(h1, j, i).start()
+            x_kv(1, j, i).start()
 
     def relay_far(j):
-        for t in range(2):
-            x_kv(1, j, t).wait_recv()
-            far_kv(1 - h1, j, t).start()
+        for i in range(PIECES):
+            x_kv(1, j, i).wait_recv()
+            far_kv(1 - h1, j, i).start()
 
     relay_near(0)
-    for t in range(2):
-        near_kv(1, t).start()
-        x_kv(2, 1, t).start()
+    for i in range(PIECES):
+        near_kv(1, i).start()
+        x_kv(2, 1, i).start()
     start(qg_copies(2))
     start(qg_copies(3))
     relay_far(0)
@@ -226,6 +243,11 @@
     first_token = 128 * p
     far_off = (1 - jnp.minimum(block // 2, 1)).astype(jnp.float32) * (-MASKED)
     near_off = (1 - jnp.minimum(block, 1)).astype(jnp.float32) * (-MASKED)
+
+    def send_first(h, j):
+        for i in range(PIECES):
+            far_s[h, j, i] = acc[(0, h, j) + at(i)].astype(jnp.bfloat16)
+            far_grad(h, j, i).start()
 
     def compute(u, between):
         h, j = order[u]
@@ -233,49 +255,47 @@
             copy.wait()
         for copy in qg_copies(u):
             copy.wait_recv()
-        for t in range(2):
-            far_kv(h, j, t).wait_recv()
+        for i in range(PIECES):
+            far_kv(h, j, i).wait_recv()
             if u in (0, 2):
-                x_kv(2, j, t).wait_recv()
+                x_kv(2, j, i).wait_recv()
         unit_grads(
-            [(kvb.at[s, h, j, 0], kvb.at[s, h, j, 1]) for s in range(3)],
+            [(kvb.at[s, h, j, pl.ds(0, 2)], kvb.at[s, h, j, pl.ds(2, 2)]) for s in range(3)],
             qb.at[h, j], gb.at[h, j], dqb.at[h, j],
             [(acc.at[s, h, j, 0], acc.at[s, h, j, 1]) for s in range(3)],
             s_ref, d_ref, first_token, far_off, near_off, between,
-        )
-        for t in range(2):
-            far_s[h, j, t] = acc[0, h, j, t].astype(jnp.bfloat16)
-            far_grad(h, j, t).start()
+            functools.partial(send_first, h, j),
+        )
         start(dq_copies(u))
 
     def send_last(j):
-        for t in range(2):
-            xs[1, j, t] = acc[2, 1 - p, j, t].astype(jnp.bfloat16)
-            x_grad(2, j, t).start()
+        for i in range(PIECES):
+            xs[1, j, i] = acc[(2, 1 - p, j) + at(i)].astype(jnp.bfloat16)
+            x_grad(2, j, i).start()
 
     def send_middle(j):
-        for t in range(2):
-            far_grad(1 - h1, j, t).wait_recv()
-            value = acc[1, 1 - h1, j, t] + far_r[1 - h1, j, t].astype(jnp.float32)
-            xs[0, j, t] = value.astype(jnp.bfloat16)
-            x_grad(1, j, t).start()
+        for i in range(PIECES):
+            far_grad(1 - h1, j, i).wait_recv()
+            value = acc[(1, 1 - h1, j) + at(i)] + far_r[1 - h1, j, i].astype(jnp.float32)
+            xs[0, j, i] = value.astype(jnp.bfloat16)
+            x_grad(1, j, i).start()
 
     def pass_on(j):
-        for t in range(2):
-            far_grad(h1, j, t).wait_recv()
-            x_grad(1, j, t).wait_recv()
-            value = acc[1, h1, j, t] + far_r[h1, j, t].astype(jnp.float32)
-            value = value + xr[0, j, t].astype(jnp.float32)
-            near_s[j, t] = value.astype(jnp.bfloat16)
-            near_grad(j, t).start()
+        for i in range(PIECES):
+            far_grad(h1, j, i).wait_recv()
+            x_grad(1, j, i).wait_recv()
+            value = acc[(1, h1, j) + at(i)] + far_r[h1, j, i].astype(jnp.float32)
+            value = value + xr[0, j, i].astype(jnp.float32)
+            near_s[j, i] = value.astype(jnp.bfloat16)
+            near_grad(j, i).start()
 
     def finish(j):
-        for t in range(2):
-            x_grad(2, j, t).wait_recv()
-            near_grad(j, t).wait_recv()
-            value = acc[2, p, j, t] + xr[1, j, t].astype(jnp.float32)
-            value = value + near_r[j, t].astype(jnp.float32)
-            wide[t, pl.ds(j, keys, stride=2)] = value
+        for i in range(PIECES):
+            x_grad(2, j, i).wait_recv()
+            near_grad(j, i).wait_recv()
+            value = acc[(2, p, j) + at(i)] + xr[1, j, i].astype(jnp.float32)
+            value = value + near_r[j, i].astype(jnp.float32)
+            wide[alternate(i, j)] = value
 
     def nothing():
         pass
@@ -291,9 +311,14 @@
     pass_on(1)
     finish(0)
     finish(1)
-    dk_out[...] = wide[0].astype(jnp.bfloat16)
-    dv_out[...] = wide[1].astype(jnp.bfloat16)
-
+    result_copies = []
+    for t, out in enumerate((dk_out, dv_out)):
+        raw[t] = wide[t].astype(jnp.bfloat16)
+        result_copies.append(pltpu.make_async_copy(raw.at[t], out, raw_sem.at[t]))
+    start(result_copies)
+
+    for copy in result_copies:
+        copy.wait()
     for u in range(4):
         own, away = dq_copies(u)
         own.wait()
@@ -302,15 +327,15 @@
         for copy in qg_copies(u):
             copy.wait_send()
     for j in range(2):
-        for t in range(2):
-            near_kv(j, t).wait_send()
-            near_grad(j, t).wait_send()
+        for i in range(PIECES):
+            near_kv(j, i).wait_send()
+            near_grad(j, i).wait_send()
             for s in (1, 2):
-                x_kv(s, j, t).wait_send()
-                x_grad(s, j, t).wait_send()
+                x_kv(s, j, i).wait_send()
+                x_grad(s, j, i).wait_send()
             for h in range(2):
-                far_kv(h, j, t).wait_send()
-                far_grad(h, j, t).wait_send()
+                far_kv(h, j, i).wait_send()
+                far_grad(h, j, i).wait_send()
 
 
 def shards(sizes, queries, key_rows, value_rows, grad_out):
@@ -319,27 +344,27 @@
     split = (tokens, 8, heads // 8, width)
     bf16, f32 = jnp.bfloat16, jnp.float32
     any_space = pl.BlockSpec(memory_space=pl.ANY)
-    vmem = pl.BlockSpec(memory_space=pltpu.VMEM)
+    hbm = pl.BlockSpec(memory_space=pltpu.HBM)
     dma = pltpu.SemaphoreType.DMA
     unit = (2, 2, 2 * tokens, heads // 8, width)
-    pieces = (2, 2, keys, width)
-    eight, four = dma((2, 2, 2)), dma((2, 2))
+    pieces = (2, PIECES, keys // 2, width)
+    many, some = dma((2, 2, PIECES)), dma((2, PIECES))
     flat = (groups * keys, width)
     dq, dk, dv = pl.pallas_call(
         functools.partial(kernel, sizes),
         out_shape=(
-            jax.ShapeDtypeStruct(split, bf16),
-            jax.ShapeDtypeStruct(flat, bf16),
-            jax.ShapeDtypeStruct(flat, bf16),
+            pltpu.VMEM(split, bf16),
+            pltpu.VMEM(flat, bf16),
+            pltpu.VMEM(flat, bf16),
         ),
-        in_specs=[any_space] * 4,
-        out_specs=(any_space, vmem, vmem),
+        in_specs=[hbm] * 4,
+        out_specs=(any_space, any_space, any_space),
         scratch_shapes=[
             pltpu.VMEM((3, 2) + pieces, bf16),
             pltpu.VMEM(unit, bf16),
             pltpu.VMEM(unit, bf16),
             pltpu.VMEM(unit, bf16),
-            pltpu.VMEM((3, 2) + pieces, f32),
+            pltpu.VMEM((3, 2, 2, 2, keys, width), f32),
             pltpu.VMEM((3, keys, ROWS), f32),
             pltpu.VMEM((3, keys, ROWS), f32),
             pltpu.VMEM((2,) + flat, bf16),
@@ -351,11 +376,13 @@
             pltpu.VMEM((2,) + pieces, bf16),
             pltpu.VMEM((2,) + pieces, bf16),
             dma((2,)), dma((4, 2)), dma((4, 2)), dma((4, 2)),
-            four, four, eight, eight, eight, eight,
+            some, some, many, many, many, many,
             dma((4,)), dma((4,)), dma((4,)),
-            eight, eight, four, four, eight, eight,
+            many, many, some, some, many, many,
         ],
-        compiler_params=pltpu.CompilerParams(collective_id=0, has_side_effects=True),
+        compiler_params=pltpu.CompilerParams(
+            collective_id=0, has_side_effects=True, vmem_limit_bytes=60 * 2**20
+        ),
         name="window_grads",
     )(
         queries.reshape(split), grad_out.reshape(split),

time: 59.9 us -> 58.1 us (0.970)
  local copies, waits for them, and re-layouts: 3.91 us -> 2.28 us
    unnamed x7 -> x3, local copies, waits for them, and re-layouts: 3.91 us -> 2.28 us
where the time goes in v3:
time: 58.1 us; the launch traced here: 58 us
  Pallas kernels  55 us (95%)
  local copies, waits for them, and re-layouts  2.28 us (4%)
  between operations  0.64 us (1%)
    pallas_call x1, Pallas kernels, shards(): pl.pallas_call(functools.partial(kernel, sizes), out_shape=(pltpu.VMEM(sp...  55 us
    unnamed x3, local copies, waits for them, and re-layouts  2.28 us

profile of v3, /device:TPU:2, one launch (start us, length us, event | category | flops | bytes accessed | tf_op | source)
XLA Modules:
  0.0 58.0 jit_solution(4236996386508823846)
XLA Ops:
  0.6 55.0 %window_grads.1 = (bf16[64,8,8,128]{3,2,1,0:T(8,128)(2,1)S(1)}, bf16[512,128]{1,0:T(8,128)(2,1)S(1)}, bf16[512,128]{1,0:T(8,128)(2,1)S(1)}) custom-call(bf16[64,8,8,128]{3,2,1,0:T(8,128)(2,1)} %bitcast.10, bf16[64,8,8,128]{3,2,1,0:T(8,128)(2,1)} %bitcast.11, bf16[512,128]{1,0:T(8,128)(2,1)} %bitcast.12, bf16[512,128]{1,0:T(8,128)(2,1)} %bitcast.13), custom_call_target="tpu_custom_call" | custom-call | tf_op jit(solution)/shard_map/window_grads/pallas_call | solution.py:353
  55.7 1.0 %copy.10 = bf16[64,64,128]{2,1,0:T(8,128)(2,1)} copy(bf16[64,64,128]{2,1,0:T(8,128)(2,1)S(1)} %bitcast.7) | data formatting | bytes 2097152
  56.6 0.7 %copy.11 = bf16[256,2,128]{2,1,0:T(2,128)(2,1)} copy(bf16[256,2,128]{2,1,0:T(2,128)(2,1)S(1)} %bitcast.9) | data formatting | bytes 262144
  57.3 0.7 %copy.12 = bf16[256,2,128]{2,1,0:T(2,128)(2,1)} copy(bf16[256,2,128]{2,1,0:T(2,128)(2,1)S(1)} %bitcast.8) | data formatting | bytes 262144

commit v4 on v3

--- a/solution.py
+++ b/solution.py
@@ -154,8 +154,8 @@
         )
 
     def x_kv(s, j, i):
-        piece = kvb.at[s, p if s == 2 else h1, j, i]
-        return remote(piece, piece, x_kv_send.at[s - 1, j, i], x_kv_recv.at[s - 1, j, i], beside)
+        piece = kvb.at[s, (a, h1, p)[s], j, i]
+        return remote(piece, piece, x_kv_send.at[s, j, i], x_kv_recv.at[s, j, i], beside)
 
     def far_grad(h, j, i):
         return remote(
@@ -227,18 +227,26 @@
             far_kv(h1, j, i).start()
             x_kv(1, j, i).start()
 
-    def relay_far(j):
-        for i in range(PIECES):
-            x_kv(1, j, i).wait_recv()
-            far_kv(1 - h1, j, i).start()
+    def second_arrivals():
+        relay_near(1)
+        for i in range(PIECES):
+            x_kv(2, 1, i).start()
+
+    def relay_far():
+        for i in range(PIECES):
+            x_kv(1, 1, i).wait_recv()
+            far_kv(1 - h1, 1, i).start()
 
     relay_near(0)
     for i in range(PIECES):
         near_kv(1, i).start()
-        x_kv(2, 1, i).start()
     start(qg_copies(2))
     start(qg_copies(3))
-    relay_far(0)
+    for i in range(PIECES):
+        far_kv(a, 0, i).wait_recv()
+        x_kv(0, 0, i).start()
+    for i in range(PIECES):
+        x_kv(1, 0, i).wait_recv()
 
     first_token = 128 * p
     far_off = (1 - jnp.minimum(block // 2, 1)).astype(jnp.float32) * (-MASKED)
@@ -256,8 +264,11 @@
         for copy in qg_copies(u):
             copy.wait_recv()
         for i in range(PIECES):
-            far_kv(h, j, i).wait_recv()
-            if u in (0, 2):
+            if u == 1:
+                x_kv(0, 0, i).wait_recv()
+            elif u > 1:
+                far_kv(h, j, i).wait_recv()
+            if j != order[u - 1][1]:
                 x_kv(2, j, i).wait_recv()
         unit_grads(
             [(kvb.at[s, h, j, pl.ds(0, 2)], kvb.at[s, h, j, pl.ds(2, 2)]) for s in range(3)],
@@ -300,8 +311,8 @@
     def nothing():
         pass
 
-    compute(0, functools.partial(relay_near, 1))
-    compute(1, functools.partial(relay_far, 1))
+    compute(0, second_arrivals)
+    compute(1, relay_far)
     send_last(0)
     compute(2, nothing)
     compute(3, functools.partial(send_middle, 0))
@@ -333,9 +344,19 @@
             for s in (1, 2):
                 x_kv(s, j, i).wait_send()
                 x_grad(s, j, i).wait_send()
+            far_kv(h1, j, i).wait_send()
+            (x_kv(0, j, i) if j == 0 else far_kv(1 - h1, j, i)).wait_send()
             for h in range(2):
-                far_kv(h, j, i).wait_send()
                 far_grad(h, j, i).wait_send()
+
+
+def write_out(*refs):
+    ins, outs, sems = refs[:3], refs[3:6], refs[6]
+    copies = [pltpu.make_async_copy(a, b, sems.at[n]) for n, (a, b) in enumerate(zip(ins, outs))]
+    for copy in copies:
+        copy.start()
+    for copy in copies:
+        copy.wait()
 
 
 def shards(sizes, queries, key_rows, value_rows, grad_out):
@@ -376,7 +397,7 @@
             pltpu.VMEM((2,) + pieces, bf16),
             pltpu.VMEM((2,) + pieces, bf16),
             dma((2,)), dma((4, 2)), dma((4, 2)), dma((4, 2)),
-            some, some, many, many, many, many,
+            some, some, many, many, dma((3, 2, PIECES)), dma((3, 2, PIECES)),
             dma((4,)), dma((4,)), dma((4,)),
             many, many, some, some, many, many,
         ],
@@ -388,6 +409,17 @@
         queries.reshape(split), grad_out.reshape(split),
         key_rows.reshape(flat), value_rows.reshape(flat),
     )
+    dq, dk, dv = pl.pallas_call(
+        write_out,
+        out_shape=(
+            pltpu.HBM(split, bf16), pltpu.HBM(flat, bf16), pltpu.HBM(flat, bf16),
+        ),
+        in_specs=[any_space] * 3,
+        out_specs=(any_space,) * 3,
+        scratch_shapes=[dma((3,))],
+        compiler_params=pltpu.CompilerParams(vmem_limit_bytes=2**20),
+        name="write_out",
+    )(dq, dk, dv)
     return dq.reshape(queries.shape), dk.reshape(key_rows.shape), dv.reshape(key_rows.shape)
 
 

time: 58.1 us -> 56.4 us (0.971)
  local copies, waits for them, and re-layouts: 2.28 us -> 0 us
  Pallas kernels: 55 us -> 55.6 us
    unnamed x3 -> x0, local copies, waits for them, and re-layouts: 2.28 us -> none
    pallas_call x0 -> x1, Pallas kernels: none -> 1.07 us  [shards(): pl.pallas_call(write_out, out_shape=(pltpu.HBM(split, bf16), pltpu.HBM(fl...]
where the time goes in v4:
time: 56.4 us; the launch traced here: 56.2 us
  Pallas kernels  55.6 us (99%)
  between operations  0.64 us (1%)
    pallas_call x1, Pallas kernels, shards(): pl.pallas_call(functools.partial(kernel, sizes), out_shape=(pltpu.VMEM(sp...  54.5 us

profile of v4, /device:TPU:2, one launch (start us, length us, event | category | flops | bytes accessed | tf_op | source)
XLA Modules:
  0.0 56.2 jit_solution(5548262612940271786)
XLA Ops:
  0.6 54.5 %window_grads.1 = (bf16[64,8,8,128]{3,2,1,0:T(8,128)(2,1)S(1)}, bf16[512,128]{1,0:T(8,128)(2,1)S(1)}, bf16[512,128]{1,0:T(8,128)(2,1)S(1)}) custom-call(bf16[64,8,8,128]{3,2,1,0:T(8,128)(2,1)} %bitcast.7, bf16[64,8,8,128]{3,2,1,0:T(8,128)(2,1)} %bitcast.8, bf16[512,128]{1,0:T(8,128)(2,1)} %bitcast.9, bf16[512,128]{1,0:T(8,128)(2,1)} %bitcast.10), custom_call_target="tpu_custom_call" | custom-call | tf_op jit(solution)/shard_map/window_grads/pallas_call | solution.py:374
  55.1 1.1 %write_out.1 = (bf16[64,8,8,128]{3,2,1,0:T(8,128)(2,1)}, bf16[512,128]{1,0:T(8,128)(2,1)}, bf16[512,128]{1,0:T(8,128)(2,1)}) custom-call(bf16[64,8,8,128]{3,2,1,0:T(8,128)(2,1)S(1)} %get-tuple-element.9.refs_0_, bf16[512,128]{1,0:T(8,128)(2,1)S(1)} %get-tuple-element.10.refs_1_, bf16[512,128]{1,0:T(8,128)(2,1)S(1)} %get-tuple-element.11.refs_2_), custom_call_target="tpu_custom_call" | custom-call | tf_op jit(solution)/shard_map/write_out/pallas_call | solution.py:412
